TPU v7x, 32 devices: a whole 2x2x4 slice. The times are simulated.
32 devices in a mesh: band: 8 (over z, core), slab: 4 (over y, x).
Axes of the slice: x: 2, y: 2, z: 4, core: 2. Of those that a mesh axis runs over, the one named last changes fastest.
Arguments:
- orbitals: float32 [9216, 24, 256], P('band', 'slab'), may hold values from -6 to 6
- rotation: float32 [9216, 512], P('band'), may hold values from -0.09375 to 0.09375
- occupation: float32 [512], P('band'), may hold values from 0.2 to 2, as said below
- metric: float32 [3, 3], replicated, may hold values from -0.3 to 1.4, as said below
Outputs:
- rotated_orbitals: float32 [512, 24, 256], P('band', 'slab')
- density: float32 [24, 16], P('slab')
Inputs may be any that keep to these rules, and one draw needn't show every extreme that they name: `occupation`: positive occupations. `metric`: symmetric with a dominant positive diagonal.
All inputs are finite; a program needn't handle non-finite values.
Results may differ from a plain program's by a relative error of at most 0.000071.
Values sent between devices are 32-bit elements; how exact they have to be, the bound alone decides.
A program may use at most 64 MiB of HBM per device.

v0:
```python
import jax
import jax.numpy as jnp
import numpy as np
from jax import lax
from jax.sharding import PartitionSpec as P

PY = 4
PX = 4


STENCIL_WEIGHTS = (6.0 / 7.0, -15.0 / 56.0, 5.0 / 63.0, -1.0 / 56.0, 6.0 / 1925.0, -1.0 / 5544.0)
HIGHEST = lax.Precision.HIGHEST


def extended(x, sides, width):
    for axis, dim in sides:
        devices, length = (lax.axis_size(axis), x.shape[dim])
        up = [(i, (i + 1) % devices) for i in range(devices)]
        down = [(j, i) for i, j in up]
        last = lax.slice_in_dim(x, length - width, length, axis=dim)
        initial = lax.slice_in_dim(x, 0, width, axis=dim)
        before = lax.ppermute(last, axis, up)
        after = lax.ppermute(initial, axis, down)
        x = jnp.concatenate([before, x, after], axis=dim)
    return x


def plane_table(count_y, count_x, along_x):
    stored_x = count_x + 12
    stored_y = count_y + 12
    table = np.zeros((stored_y * stored_x, count_y * count_x), np.float32)
    for row_y in range(count_y):
        for row_x in range(count_x):
            target = row_y * count_x + row_x
            for distance, weight in enumerate(STENCIL_WEIGHTS, start=1):
                if along_x:
                    ahead = (row_y + 6) * stored_x + row_x + 6 + distance
                    behind = (row_y + 6) * stored_x + row_x + 6 - distance
                else:
                    ahead = (row_y + 6 + distance) * stored_x + row_x + 6
                    behind = (row_y + 6 - distance) * stored_x + row_x + 6
                table[ahead, target] += weight
                table[behind, target] -= weight
    return jnp.asarray(table)


def density_part(field_rows, weights, metric, table_x, table_y):
    row_count, depth_cells, plane_size = field_rows.shape
    stored_x = PX + 12
    grid_view = field_rows.reshape(row_count, depth_cells, PY + 12, stored_x)
    interior = grid_view[:, :, 6 : 6 + PY, 6 : 6 + PX].reshape(row_count, depth_cells, PY * PX)
    padded = extended(interior, (("slab", 1),), 6)
    grad_z = jnp.zeros_like(interior)
    for distance, weight in enumerate(STENCIL_WEIGHTS, start=1):
        grad_z = grad_z + weight * (
            padded[:, 6 + distance : 6 + distance + depth_cells]
            - padded[:, 6 - distance : 6 - distance + depth_cells]
        )
    flattened = field_rows.reshape(row_count * depth_cells, plane_size)
    grad_x = jnp.dot(
        flattened, table_x, precision=HIGHEST, preferred_element_type=jnp.float32
    ).reshape(interior.shape)
    grad_y = jnp.dot(
        flattened, table_y, precision=HIGHEST, preferred_element_type=jnp.float32
    ).reshape(interior.shape)
    components = (grad_x, grad_y, grad_z)
    quadratic = jnp.zeros_like(interior)
    for left_axis in range(3):
        for right_axis in range(3):
            quadratic = (
                quadratic
                + metric[left_axis, right_axis] * components[left_axis] * components[right_axis]
            )
    return jnp.einsum(
        "r,rc->c", weights, quadratic.reshape(row_count, depth_cells * PY * PX), precision=HIGHEST
    )


def local(orbitals, rotation, occupation, metric):
    band_count = lax.axis_size("band")
    local_orbitals, depth_cells, plane_size = orbitals.shape
    window = rotation.shape[1]
    owned = window // band_count
    flattened = orbitals.reshape(local_orbitals, depth_cells * plane_size)
    table_x = plane_table(PY, PX, True)
    table_y = plane_table(PY, PX, False)
    rotated = lax.psum_scatter(
        lax.dot_general(
            rotation,
            flattened,
            (((0,), (0,)), ((), ())),
            precision=HIGHEST,
            preferred_element_type=jnp.float32,
        ),
        "band",
        scatter_dimension=0,
        tiled=True,
    )
    rotated = rotated.reshape(owned, depth_cells, plane_size)
    partial_density = density_part(rotated, occupation, metric, table_x, table_y)
    summed = lax.psum(partial_density, "band")
    density = (summed * (0.5 / window)).reshape(depth_cells, PY * PX)
    return (rotated, density)


def solution(mesh):
    placed = (P("band", "slab", None), P("band", None), P("band"), P())
    return jax.shard_map(
        local,
        mesh=mesh,
        in_specs=placed,
        out_specs=(P("band", "slab", None), P("slab", None)),
        check_vma=False,
    )
```

profile of v0, /device:TPU:0, one launch (start us, length us, event | category | flops | bytes accessed | tf_op | source)
XLA Modules:
  0.0 120.8 jit_solution(6772078114257280988)
XLA Ops:
  7.2 0.0 copy-start
  7.2 0.0 reduce-scatter.2.cloned.1.call-start
  7.2 8.3 %copy.12 = f32[1152,6,256]{0,2,1:T(8,128)} copy(f32[1152,6,256]{2,0,1:T(8,128)} %param.6) | data formatting | bytes 14155776 | tf_op args[0]
  15.5 0.0 copy-done
  15.5 25.6 %fusion.33 = f32[512,1536]{1,0:T(8,128)} fusion(f32[1152,512]{1,0:T(8,128)S(1)} %copy-done, f32[1152,1536]{0,1:T(8,128)} %bitcast.31), kind=kOutput, calls=%fused_computation.57 | convolution fusion | flops 10871635968 | bytes 12582912 | tf_op jit(solution)/shard_map/dot_general | solution.py:88
  41.1 0.0 copy-start.3
  41.1 0.0 copy-start.2
  41.1 0.0 copy-start.5
  41.1 0.0 copy-start.4
  41.1 0.0 reduce-scatter.2.cloned.1.call-update
  41.2 0.6 copy-done.3
  41.8 0.7 fusion.32
  42.5 41.9 %reduce-scatter.2.cloned.1.call-done = f32[64,1536]{1,0:T(8,128)} async-done(((f32[512,1536]{1,0:T(8,128)}), f32[64,1536]{1,0:T(8,128)}) %reduce-scatter.2.cloned.1.call-update) | async-done | bytes 393232 | tf_op jit(solution)/shard_map/reduce_scatter | solution.py:87
  84.4 1.3 %copy.15 = f32[64,1536]{0,1:T(8,128)S(1)} copy(f32[64,1536]{1,0:T(8,128)} %reduce-scatter.2.cloned.1.call-done) | data formatting | bytes 786432 | tf_op jit(solution)/shard_map/reduce_scatter | solution.py:87
  85.6 2.4 %collective-permute-start = (f32[64,6,16]{0,2,1:T(8,128)S(1)}, f32[64,6,16]{0,2,1:T(8,128)S(1)}, u32[]{:S(2)}, u32[]{:S(2)}) collective-permute-start(f32[64,6,16]{0,2,1:T(8,128)S(1)} %bitcast.37), channel_id=1, source_target_pairs={{1,0},{2,1},{3,2},{0,3},{5,4},{6,5},{7,6},{4,7},{9,8},{10,9},{11,1... | collective-permute-start | bytes 73736 | tf_op jit(solution)/shard_map/ppermute | solution.py:23
  88.1 0.0 collective-permute-start.1
  88.1 1.0 copy.19
  89.1 0.0 copy-start.1
  89.1 0.0 copy-done.2
  89.1 0.6 fusion.34
  89.7 0.1 collective-permute-done
  89.8 3.2 %collective-permute-done.1 = f32[64,6,16]{0,2,1:T(8,128)S(1)} collective-permute-done((f32[64,6,16]{0,2,1:T(8,128)S(1)}, f32[64,6,16]{0,2,1:T(8,128)S(1)}, u32[]{:S(2)}, u32[]{:S(2)}) %collective-permute-start.1) | collective-permute-done | bytes 24608 | tf_op jit(solution)/shard_map/ppermute | solution.py:22
  93.0 0.0 copy-done.5
  93.0 6.3 %fusion.7 = f32[64,6,16]{0,2,1:T(8,128)S(1)} fusion(f32[64,6,16]{0,2,1:T(8,128)S(1)} %fusion.34, f32[64,6,16]{0,2,1:T(8,128)S(1)} %collective-permute-done, f32[64,6,16]{0,2,1:T(8,128)S(1)} %collective-permute-done.1, f32[64,6,16]{0,2,1:T(8,128)S(1)} %bitcast.39, f32[]{:T(128)} %bitcast.13, f32[]{:T(128)} %bitcast.12, f32[]{:T(128)} %bitcast.11, ...), kind=kOutput, calls=%fused_computation.28 | convolution fusion | flops 19200000 | bytes 532516 | tf_op jit(solution)/shard_map/dot_general | solution.py:60
  99.3 0.0 copy-done.4
  99.3 0.2 convolution_bitcast_fusion
  99.5 13.7 %psum.7 = f32[96]{0:T(128)S(1)} all-reduce(f32[96]{0:T(128)S(1)} %convolution_bitcast_fusion), channel_id=1, replica_groups=mesh['band'=8,'slab'=4] {'band'}, use_global_device_ids=true, to_apply=%region_1.0 | all-reduce | flops 96 | bytes 768 | tf_op jit(solution)/shard_map/psum | solution.py:101
  113.2 0.7 reshape.29
  113.9 0.0 copy-done.1
  (2 shorter events, 0.0 us)
Async XLA Ops:
  7.2 8.4 %copy-start = (f32[1152,512]{1,0:T(8,128)S(1)}, f32[1152,512]{1,0:T(8,128)}, u32[]{:S(2)}) copy-start(f32[1152,512]{1,0:T(8,128)} %param.7) | copy-start | bytes 7077892
  7.2 77.2 %reduce-scatter.2.cloned.1.call-start = ((), (), s32[]{:S(2)}) async-start(), calls=%async_computation.1 | async-start | bytes 3538944 | tf_op jit(solution)/shard_map/reduce_scatter | solution.py:87
  41.1 0.7 copy-start.3
  41.1 48.0 %copy-start.2 = (f32[256,16,1]{0,1,2:T(8,128)S(1)}, f32[256,16,1]{0,1,2:T(8,128)}, u32[]{:S(2)}) copy-start(f32[256,16,1]{0,1,2:T(8,128)} %constant.22) | copy-start | bytes 49156
  41.1 51.9 %copy-start.5 = (f32[256,16,1]{0,1,2:T(8,128)S(1)}, f32[256,16,1]{0,1,2:T(8,128)}, u32[]{:S(2)}) copy-start(f32[256,16,1]{0,1,2:T(8,128)} %constant.21) | copy-start | bytes 49156
  41.1 58.2 %copy-start.4 = (f32[64]{0:T(128)S(1)}, f32[64]{0:T(128)}, u32[]{:S(2)}) copy-start(f32[64]{0:T(128)} %param.8) | copy-start | bytes 772
  85.6 4.2 %collective-permute-start = (f32[64,6,16]{0,2,1:T(8,128)S(1)}, f32[64,6,16]{0,2,1:T(8,128)S(1)}, u32[]{:S(2)}, u32[]{:S(2)}) collective-permute-start(f32[64,6,16]{0,2,1:T(8,128)S(1)} %bitcast.37), channel_id=1, source_target_pairs={{1,0},{2,1},{3,2},{0,3},{5,4},{6,5},{7,6},{4,7},{9,8},{10,9},{11,1... | collective-permute-start | bytes 73736 | tf_op jit(solution)/shard_map/ppermute | solution.py:23
  88.1 5.0 %collective-permute-start.1 = (f32[64,6,16]{0,2,1:T(8,128)S(1)}, f32[64,6,16]{0,2,1:T(8,128)S(1)}, u32[]{:S(2)}, u32[]{:S(2)}) collective-permute-start(f32[64,6,16]{0,2,1:T(8,128)S(1)} %bitcast.38), channel_id=1, source_target_pairs={{0,1},{1,2},{2,3},{3,0},{4,5},{5,6},{6,7},{7,4},{8,9},{9,10},{10,1... | collective-permute-start | bytes 73736 | tf_op jit(solution)/shard_map/ppermute | solution.py:22
  89.1 24.8 %copy-start.1 = (f32[8,6,8,256]{3,2,0,1:T(8,128)}, f32[8,6,8,256]{3,2,0,1:T(8,128)S(1)}, u32[]{:S(2)}) copy-start(f32[8,6,8,256]{3,2,0,1:T(8,128)S(1)} %copy.19) | copy-start | bytes 1179652
Sparse Core Ops, SparseCore 0:
  41.3 43.0 reduce-scatter.1
where the time goes:
time: 121 us
  waiting for transfers between devices  45.3 us (37%)
  matrix products  32.6 us (27%)
  between operations  14.1 us (12%)
  blocking collectives  13.7 us (11%)
  local copies, waits for them, and re-layouts  12.6 us (10%)
  starting transfers between devices  2.45 us (2%)
    reduce_scatter x1, waiting for transfers between devices, local(): lax.psum_scatter(lax.dot_general(rotation, flattened, (((0,), (0,)), ((),...  41.9 us
    dot_general x1, matrix products, local(): lax.dot_general(rotation, flattened, (((0,), (0,)), ((), ())), precision=...  25.6 us
    psum x1, blocking collectives, local(): summed = lax.psum(partial_density, 'band')  13.7 us
    unnamed x13, local copies, waits for them, and re-layouts  8.98 us
    dot_general x1, matrix products, density_part(): jnp.dot(flattened, table_x, precision=HIGHEST, preferred_element_type=jnp...  6.25 us
    ppermute x1, waiting for transfers between devices, extended(): before = lax.ppermute(last, axis, up)  3.24 us
  transfers between devices with their start and end apart: 3, of which 3 were waited for; matrix products, arithmetic and copies ran while one was open for 2% of the time, Pallas kernels for 0%

commit v1 on v0

v1 whole, which is shorter than its diff:
```python
import functools

import jax
import jax.numpy as jnp
import numpy as np
from jax import lax
from jax.experimental import pallas as pl
from jax.experimental.pallas import tpu as pltpu
from jax.sharding import PartitionSpec as P

PY = 4
PX = 4
LANES = 128
REACH = 6
MESH = pl.DeviceIdType.MESH
STENCIL_WEIGHTS = (6.0 / 7.0, -15.0 / 56.0, 5.0 / 63.0, -1.0 / 56.0, 6.0 / 1925.0, -1.0 / 5544.0)
HIGHEST = lax.Precision.HIGHEST


def plane_tables():
    stored_x = PX + 12
    table = np.zeros(((PY + 12) * stored_x, 3 * LANES), np.float32)
    for row_y in range(PY):
        for row_x in range(PX):
            point = row_y * PX + row_x
            centre = (row_y + 6) * stored_x + row_x + 6
            table[centre, point] = 1.0
            for distance, weight in enumerate(STENCIL_WEIGHTS, start=1):
                table[centre + distance, LANES + point] += weight
                table[centre - distance, LANES + point] -= weight
                table[centre + distance * stored_x, 2 * LANES + point] += weight
                table[centre - distance * stored_x, 2 * LANES + point] -= weight
    return table


def depth_tables(planes, hops):
    points = PY * PX
    table = np.zeros((2 * hops + 1, LANES, LANES), np.float32)
    for plane in range(planes):
        for distance, weight in enumerate(STENCIL_WEIGHTS, start=1):
            for signed, value in ((distance, weight), (-distance, -weight)):
                slab, source = divmod(plane + signed, planes)
                for point in range(points):
                    table[slab + hops, source * points + point, plane * points + point] += value
    return table


def kernel(
    sizes, orb_hbm, rot_hbm, occ_ref, metric_ref, plane_ref, depth_ref, out_ref, dens_ref,
    orb, rot, left, part, crecv, sbuf, line, halo, terms,
    orb_sem, rot_sem, core_send, core_recv, line_send, line_recv, halo_send, halo_recv, term_send, term_recv,
):
    bands, slabs, planes, owned, hops, window = sizes
    chips = bands // 2
    me, slab = lax.axis_index("band"), lax.axis_index("slab")
    chip, core = me // 2, me % 2
    partner = (chip * 2 + 1 - core, slab)
    ahead, behind = (me + 2, slab), (me - 2, slab)

    def load(p):
        return pltpu.make_async_copy(orb_hbm.at[p], orb.at[p], orb_sem.at[p])

    load_rot = pltpu.make_async_copy(rot_hbm, rot, rot_sem)
    load_rot.start()
    for p in range(planes):
        load(p).start()

    barrier = pltpu.get_barrier_semaphore()
    for k in range(1, bands):
        pl.semaphore_signal(barrier, inc=1, device_id=((me + k) % bands, slab), device_id_type=MESH)
    offsets = [h for h in range(-hops, hops + 1) if h != 0]
    for h in offsets:
        pl.semaphore_signal(barrier, inc=1, device_id=(me, (slab + h + slabs) % slabs), device_id_type=MESH)

    load_rot.wait()
    for chip_at in range(chips):
        rows = jnp.transpose(rot[:, chip_at * 2 * owned : (chip_at + 1) * 2 * owned])
        high = rows.astype(jnp.bfloat16)
        low = (rows - high.astype(jnp.float32)).astype(jnp.bfloat16)
        for core_at in range(2):
            at = (core_at * chips + chip_at) * owned
            left[at : at + owned, :] = high[core_at * owned : (core_at + 1) * owned]
            left[window + at : window + at + owned, :] = low[core_at * owned : (core_at + 1) * owned]

    def core_copy(p):
        return pltpu.make_async_remote_copy(
            src_ref=part.at[p, 1 - core], dst_ref=crecv.at[p], send_sem=core_send.at[p], recv_sem=core_recv.at[p],
            device_id=partner, device_id_type=MESH,
        )

    def multiply(p):
        load(p).wait()
        field = orb[p]
        high = field.astype(jnp.bfloat16)
        low = (field - high.astype(jnp.float32)).astype(jnp.bfloat16)
        both = jnp.dot(left[...], high, preferred_element_type=jnp.float32)
        small = jnp.dot(left[:window, :], low, preferred_element_type=jnp.float32)
        total = both[:window] + (both[window:] + small)
        part[p] = total.reshape(2, window // 2, total.shape[-1])

    def line_copy(direction, p, t, src, target):
        return pltpu.make_async_remote_copy(
            src_ref=src, dst_ref=line.at[direction, p, t],
            send_sem=line_send.at[direction, p, t], recv_sem=line_recv.at[direction, p, t],
            device_id=target, device_id_type=MESH,
        )

    def block(d):
        return pl.ds(pl.multiple_of(d * owned, owned), owned)

    def originate(p):
        core_copy(p).wait_recv()
        sbuf[p] = part[p, core] + crecv[p]
        for t in range(chips - 1):
            @pl.when(chip == 0)
            def _():
                line_copy(0, p, t, sbuf.at[p, block(chips - 1 - t)], ahead).start()

            @pl.when(chip == chips - 1)
            def _():
                line_copy(1, p, t, sbuf.at[p, block(t)], behind).start()
        out_ref[p] = sbuf[p, block(chip), :]

    def forward(p):
        def rightward(t):
            @pl.when((chip > 0) & (chip < chips - 1 - t))
            def _():
                line_copy(0, p, t, line.at[0, p, t], behind).wait_recv()
                line[0, p, t] += sbuf[p, block(chips - 1 - t), :]
                line_copy(0, p, t, line.at[0, p, t], ahead).start()

        def leftward(t):
            @pl.when((chip < chips - 1) & (chip > t))
            def _():
                line_copy(1, p, t, line.at[1, p, t], ahead).wait_recv()
                line[1, p, t] += sbuf[p, block(t), :]
                line_copy(1, p, t, line.at[1, p, t], behind).start()

        @pl.when(chip < chips // 2)
        def _():
            for t in range(chips - 1):
                rightward(t)
            for t in range(chips - 1):
                leftward(t)

        @pl.when(chip >= chips // 2)
        def _():
            for t in range(chips - 1):
                leftward(t)
            for t in range(chips - 1):
                rightward(t)

        @pl.when(chip > 0)
        def _():
            t = chips - 1 - chip
            line_copy(0, p, t, line.at[0, p, t], behind).wait_recv()
            out_ref[p] += line[0, p, t]

        @pl.when(chip < chips - 1)
        def _():
            line_copy(1, p, chip, line.at[1, p, chip], ahead).wait_recv()
            out_ref[p] += line[1, p, chip]

    multiply(0)
    pl.semaphore_wait(barrier, bands - 1 + len(offsets))
    core_copy(0).start()

    def step(p, carry):
        multiply(p)
        core_copy(p).start()
        originate(p - 1)
        return carry

    lax.fori_loop(1, planes, step, 0)
    originate(planes - 1)

    def onward(p, carry):
        forward(p)
        return carry

    lax.fori_loop(0, planes, onward, 0)

    points = PY * PX
    table = plane_ref[...]
    values = jnp.zeros((owned, 3 * LANES), jnp.float32)
    for p in range(planes):
        part_values = jnp.dot(out_ref[p], table, precision=HIGHEST, preferred_element_type=jnp.float32)
        if p:
            part_values = jnp.concatenate(
                [pltpu.roll(part_values[:, g * LANES : (g + 1) * LANES], p * points, 1) for g in range(3)], axis=1
            )
        values = values + part_values
    halo[hops] = values[:, :LANES]
    grad_x = values[:, LANES : 2 * LANES]
    grad_y = values[:, 2 * LANES :]

    def halo_copy(number, h):
        return pltpu.make_async_remote_copy(
            src_ref=halo.at[hops], dst_ref=halo.at[hops - h],
            send_sem=halo_send.at[number], recv_sem=halo_recv.at[number],
            device_id=(me, (slab + h + slabs) % slabs), device_id_type=MESH,
        )

    copies = [halo_copy(number, h) for number, h in enumerate(offsets)]
    for copy in copies:
        copy.start()
    grad_z = jnp.dot(halo[hops], depth_ref[hops], precision=HIGHEST, preferred_element_type=jnp.float32)
    for copy, h in zip(copies, offsets):
        copy.wait()
        grad_z = grad_z + jnp.dot(
            halo[hops - h], depth_ref[hops - h], precision=HIGHEST, preferred_element_type=jnp.float32
        )
    components = (grad_x, grad_y, grad_z)
    quadratic = jnp.zeros_like(grad_x)
    for i in range(3):
        for j in range(3):
            quadratic = quadratic + metric_ref[i, j] * components[i] * components[j]
    term = jnp.dot(occ_ref[...], quadratic, precision=HIGHEST, preferred_element_type=jnp.float32)
    terms[me] = jnp.broadcast_to(term, (8, LANES))

    def term_copy(k):
        return pltpu.make_async_remote_copy(
            src_ref=terms.at[me], dst_ref=terms.at[me],
            send_sem=term_send.at[k - 1], recv_sem=term_recv.at[k - 1],
            device_id=((me + k) % bands, slab), device_id_type=MESH,
        )

    for k in range(1, bands):
        term_copy(k).start()

    def sent(p, carry):
        core_copy(p).wait_send()
        for t in range(chips - 1):
            @pl.when(chip < chips - 1 - t)
            def _():
                line_copy(0, p, t, line.at[0, p, t], ahead).wait_send()

            @pl.when(chip > t)
            def _():
                line_copy(1, p, t, line.at[1, p, t], behind).wait_send()
        return carry

    lax.fori_loop(0, planes, sent, 0)
    for k in range(1, bands):
        term_copy(k).wait()
    summed = terms[0]
    for b in range(1, bands):
        summed = summed + terms[b]
    summed = summed * (0.5 / window)
    for p in range(planes):
        dens_ref[p : p + 1, :] = summed[0:1, p * points : (p + 1) * points]


def local(orbitals, rotation, occupation, metric):
    bands, slabs = lax.axis_size("band"), lax.axis_size("slab")
    orbital_count, planes, plane_size = orbitals.shape
    window = rotation.shape[1]
    owned = window // bands
    chips = bands // 2
    hops = -(-REACH // planes)
    f32 = jnp.float32
    vmem = pl.BlockSpec(memory_space=pltpu.VMEM)
    hbm = pl.BlockSpec(memory_space=pl.ANY)
    dma = pltpu.SemaphoreType.DMA
    neighbours = 2 * hops
    rotated, density = pl.pallas_call(
        functools.partial(kernel, (bands, slabs, planes, owned, hops, window)),
        out_shape=(
            jax.ShapeDtypeStruct((planes, owned, plane_size), f32),
            jax.ShapeDtypeStruct((planes, PY * PX), f32),
        ),
        in_specs=[hbm, hbm, vmem, pl.BlockSpec(memory_space=pltpu.SMEM), vmem, vmem],
        out_specs=(vmem, vmem),
        scratch_shapes=[
            pltpu.VMEM((planes, orbital_count, plane_size), f32),
            pltpu.VMEM((orbital_count, window), f32),
            pltpu.VMEM((2 * window, orbital_count), jnp.bfloat16),
            pltpu.VMEM((planes, 2, window // 2, plane_size), f32),
            pltpu.VMEM((planes, window // 2, plane_size), f32),
            pltpu.VMEM((planes, window // 2, plane_size), f32),
            pltpu.VMEM((2, planes, chips - 1, owned, plane_size), f32),
            pltpu.VMEM((neighbours + 1, owned, LANES), f32),
            pltpu.VMEM((bands, 8, LANES), f32),
            dma((planes,)),
            dma,
            dma((planes,)),
            dma((planes,)),
            dma((2, planes, chips - 1)),
            dma((2, planes, chips - 1)),
            dma((neighbours,)),
            dma((neighbours,)),
            dma((bands - 1,)),
            dma((bands - 1,)),
        ],
        compiler_params=pltpu.CompilerParams(
            collective_id=0, has_side_effects=True, vmem_limit_bytes=48 * 1024 * 1024
        ),
    )(
        jnp.transpose(orbitals, (1, 0, 2)),
        rotation,
        occupation.reshape(1, owned),
        metric,
        jnp.asarray(plane_tables()),
        jnp.asarray(depth_tables(planes, hops)),
    )
    return jnp.transpose(rotated, (1, 0, 2)), density


def solution(mesh):
    placed = (P("band", "slab", None), P("band", None), P("band"), P())
    return jax.shard_map(
        local,
        mesh=mesh,
        in_specs=placed,
        out_specs=(P("band", "slab", None), P("slab", None)),
        check_vma=False,
    )
```

time: 121 us -> 61 us (0.50)
  Pallas kernels: 0 us -> 53.9 us
  waiting for transfers between devices: 45.3 us -> 0 us
  matrix products: 32.6 us -> 0 us
  blocking collectives: 13.7 us -> 0 us
  between operations: 14.1 us -> 0.65 us
  local copies, waits for them, and re-layouts: 12.6 us -> 6.26 us
  starting transfers between devices: 2.45 us -> 0 us
    pallas_call x0 -> x1, Pallas kernels: none -> 53.9 us  [local(): pl.pallas_call(functools.partial(kernel, (bands, slabs, planes, owned, ho...]
    reduce_scatter x1 -> x0, waiting for transfers between devices: 41.9 us -> none  [local(): lax.psum_scatter(lax.dot_general(rotation, flattened, (((0,), (0,)), ((),...]
    dot_general x4 -> x0, matrix products: 32.6 us -> none  [the longest x1 25.6 us: local(): lax.dot_general(rotation, flattened, (((0,), (0,)), ((), ())), precision=...]
    psum x1 -> x0, blocking collectives: 13.7 us -> none  [local(): summed = lax.psum(partial_density, 'band')]
    ppermute x2 -> x0, waiting for transfers between devices: 3.37 us -> none  [the longest x1 3.24 us: extended(): before = lax.ppermute(last, axis, up)]
    unnamed x13 -> x12, local copies, waits for them, and re-layouts: 8.98 us -> 6.26 us
    ppermute x2 -> x0, starting transfers between devices: 2.41 us -> none  [the longest x1 2.41 us: extended(): after = lax.ppermute(initial, axis, down)]
    reshape x2 -> x0, local copies, waits for them, and re-layouts: 1.7 us -> none  [the longest x1 1.02 us: local(): rotated = rotated.reshape(owned, depth_cells, plane_size)]
  transfers between devices with their start and end apart: 3 -> 0, of which waited for: 3 -> 0; matrix products, arithmetic and copies ran while one was open for 2% -> 0% of each run, Pallas kernels for 0% -> 0%
where the time goes in v1:
time: 61 us; the launch traced here: 60.8 us
  Pallas kernels  53.9 us (88%)
  local copies, waits for them, and re-layouts  6.26 us (10%)
  between operations  0.65 us (1%)
    pallas_call x1, Pallas kernels, local(): pl.pallas_call(functools.partial(kernel, (bands, slabs, planes, owned, ho...  53.9 us
    unnamed x12, local copies, waits for them, and re-layouts  6.26 us

profile of v1, /device:TPU:0, one launch (start us, length us, event | category | flops | bytes accessed | tf_op | source)
XLA Modules:
  0.0 60.8 jit_solution(3341637470368348052)
XLA Ops:
  0.6 0.0 copy-start
  0.6 1.7 %copy-done = f32[1152,512]{1,0:T(8,128)S(1)} copy-done((f32[1152,512]{1,0:T(8,128)S(1)}, f32[1152,512]{1,0:T(8,128)}, u32[]{:S(2)}) %copy-start) | copy-done | bytes 2359320
  2.3 0.0 copy-start.1
  2.3 1.0 %copy-done.1 = f32[256,384]{1,0:T(8,128)S(1)} copy-done((f32[256,384]{1,0:T(8,128)S(1)}, f32[256,384]{1,0:T(8,128)}, u32[]{:S(2)}) %copy-start.1) | copy-done | bytes 393240
  3.3 0.0 copy-start.2
  3.3 0.9 %copy-done.2 = f32[3,128,128]{2,1,0:T(8,128)S(1)} copy-done((f32[3,128,128]{2,1,0:T(8,128)S(1)}, f32[3,128,128]{2,1,0:T(8,128)}, u32[]{:S(2)}) %copy-start.2) | copy-done | bytes 196632
  4.2 0.0 copy-start.3
  4.2 0.7 %copy-done.3 = f32[3,3]{1,0:T(4,128)S(1)} copy-done((f32[3,3]{1,0:T(4,128)S(1)}, f32[3,3]{1,0:T(4,128)}, u32[]{:S(2)}) %copy-start.3) | copy-done | bytes 60
  4.9 0.0 copy-start.4
  4.9 0.7 %copy-done.4 = f32[64]{0:T(128)S(1)} copy-done((f32[64]{0:T(128)S(1)}, f32[64]{0:T(128)}, u32[]{:S(2)}) %copy-start.4) | copy-done | bytes 280
  5.6 53.9 %shard_map.77 = (f32[6,64,256]{2,1,0:T(8,128)S(1)}, f32[6,16]{1,0:T(8,128)S(1)}) custom-call(f32[6,1152,256]{2,1,0:T(8,128)} %bitcast.5, f32[1152,512]{1,0:T(8,128)S(1)} %copy-done, f32[1,64]{1,0:T(1,128)S(1)} %bitcast.4, f32[3,3]{1,0:T(4,128)S(1)} %copy-done.3, f32[256,384]{1,0:T(8,128)S(1)} %copy-done.1, f32[3,128,128]{2,1,0:T(8,128)S(1)} %copy-done.2), custom_call_target="tpu_custom_call" | custom-call | tf_op jit(solution)/shard_map/pallas_call | solution.py:266
  59.4 0.7 %copy.10 = f32[64,6,256]{2,0,1:T(8,128)} copy(f32[64,6,256]{2,0,1:T(8,128)S(1)} %bitcast.3) | data formatting | bytes 786432
  60.2 0.6 copy.11
Async XLA Ops:
  0.6 1.7 %copy-start = (f32[1152,512]{1,0:T(8,128)S(1)}, f32[1152,512]{1,0:T(8,128)}, u32[]{:S(2)}) copy-start(f32[1152,512]{1,0:T(8,128)} %rot_hbm.1) | copy-start | bytes 7077892
  2.3 1.0 %copy-start.1 = (f32[256,384]{1,0:T(8,128)S(1)}, f32[256,384]{1,0:T(8,128)}, u32[]{:S(2)}) copy-start(f32[256,384]{1,0:T(8,128)} %constant.4.clone.plane_ref) | copy-start | bytes 1179652
  3.3 0.9 %copy-start.2 = (f32[3,128,128]{2,1,0:T(8,128)S(1)}, f32[3,128,128]{2,1,0:T(8,128)}, u32[]{:S(2)}) copy-start(f32[3,128,128]{2,1,0:T(8,128)} %constant.5.clone.depth_ref) | copy-start | bytes 589828
  4.2 0.7 %copy-start.3 = (f32[3,3]{1,0:T(4,128)S(1)}, f32[3,3]{1,0:T(4,128)}, u32[]{:S(2)}) copy-start(f32[3,3]{1,0:T(4,128)} %metric_ref.1) | copy-start | bytes 112
  4.9 0.7 %copy-start.4 = (f32[64]{0:T(128)S(1)}, f32[64]{0:T(128)}, u32[]{:S(2)}) copy-start(f32[64]{0:T(128)} %param.8) | copy-start | bytes 772

commit v2 on v1

--- a/solution.py
+++ b/solution.py
@@ -2,6 +2,7 @@
 
 import jax
 import jax.numpy as jnp
+import ml_dtypes
 import numpy as np
 from jax import lax
 from jax.experimental import pallas as pl
@@ -45,15 +46,32 @@
     return table
 
 
+def split_dot(x, table):
+    depth = x.shape[1]
+    high = x.astype(jnp.bfloat16)
+    low = (x - high.astype(jnp.float32)).astype(jnp.bfloat16)
+    f32 = jnp.float32
+    main = jnp.dot(high, table[:depth], preferred_element_type=f32)
+    rest = jnp.dot(low, table[:depth], preferred_element_type=f32)
+    return main + (rest + jnp.dot(high, table[depth:], preferred_element_type=f32))
+
+
+def halves(table):
+    high = table.astype(ml_dtypes.bfloat16)
+    low = (table - high.astype(np.float32)).astype(ml_dtypes.bfloat16)
+    return jnp.asarray(np.concatenate([high, low], axis=0))
+
+
 def kernel(
-    sizes, orb_hbm, rot_hbm, occ_ref, metric_ref, plane_ref, depth_ref, out_ref, dens_ref,
-    orb, rot, left, part, crecv, sbuf, line, halo, terms,
+    sizes, orb_hbm, rot_hbm, occ_hbm, metric_hbm, plane_hbm, depth_hbm, out_ref, dens_ref,
+    occ_ref, metric_ref, plane_ref, depth_ref, values, small_sem, orb, rot, left, part, crecv, sbuf, line, halo, terms,
     orb_sem, rot_sem, core_send, core_recv, line_send, line_recv, halo_send, halo_recv, term_send, term_recv,
 ):
     bands, slabs, planes, owned, hops, window = sizes
     chips = bands // 2
     me, slab = lax.axis_index("band"), lax.axis_index("slab")
     chip, core = me // 2, me % 2
+    points = PY * PX
     partner = (chip * 2 + 1 - core, slab)
     ahead, behind = (me + 2, slab), (me - 2, slab)
 
@@ -64,6 +82,14 @@
     load_rot.start()
     for p in range(planes):
         load(p).start()
+    small_loads = [
+        pltpu.make_async_copy(src, dst, small_sem.at[n])
+        for n, (src, dst) in enumerate(
+            ((occ_hbm, occ_ref), (metric_hbm, metric_ref), (plane_hbm, plane_ref), (depth_hbm, depth_ref))
+        )
+    ]
+    for small_load in small_loads:
+        small_load.start()
 
     barrier = pltpu.get_barrier_semaphore()
     for k in range(1, bands):
@@ -114,14 +140,22 @@
         for t in range(chips - 1):
             @pl.when(chip == 0)
             def _():
+                @pl.when(p > 0)
+                def _():
+                    line_copy(0, p - 1, t, sbuf.at[p - 1, block(chips - 1 - t)], ahead).wait_send()
+
                 line_copy(0, p, t, sbuf.at[p, block(chips - 1 - t)], ahead).start()
 
             @pl.when(chip == chips - 1)
             def _():
+                @pl.when(p > 0)
+                def _():
+                    line_copy(1, p - 1, t, sbuf.at[p - 1, block(t)], behind).wait_send()
+
                 line_copy(1, p, t, sbuf.at[p, block(t)], behind).start()
         out_ref[p] = sbuf[p, block(chip), :]
 
-    def forward(p):
+    def transit(p):
         def rightward(t):
             @pl.when((chip > 0) & (chip < chips - 1 - t))
             def _():
@@ -150,6 +184,7 @@
             for t in range(chips - 1):
                 rightward(t)
 
+    def finish(p):
         @pl.when(chip > 0)
         def _():
             t = chips - 1 - chip
@@ -161,35 +196,46 @@
             line_copy(1, p, chip, line.at[1, p, chip], ahead).wait_recv()
             out_ref[p] += line[1, p, chip]
 
+        found = split_dot(out_ref[p], plane_ref[...])
+        for g in range(3):
+            group = found[:, g * LANES : (g + 1) * LANES]
+            values[:, g * LANES : (g + 1) * LANES] += pltpu.roll(group, p * points, 1)
+
     multiply(0)
     pl.semaphore_wait(barrier, bands - 1 + len(offsets))
     core_copy(0).start()
+    values[...] = jnp.zeros_like(values)
+    for small_load in small_loads:
+        small_load.wait()
 
     def step(p, carry):
         multiply(p)
         core_copy(p).start()
         originate(p - 1)
+
+        @pl.when(p >= 2)
+        def _():
+            transit(p - 2)
+
+        @pl.when(p >= 3)
+        def _():
+            finish(p - 3)
+
         return carry
 
     lax.fori_loop(1, planes, step, 0)
     originate(planes - 1)
 
-    def onward(p, carry):
-        forward(p)
+    def drain(p, carry):
+        transit(p)
+        finish(p - 1)
         return carry
 
-    lax.fori_loop(0, planes, onward, 0)
-
-    points = PY * PX
-    table = plane_ref[...]
-    values = jnp.zeros((owned, 3 * LANES), jnp.float32)
-    for p in range(planes):
-        part_values = jnp.dot(out_ref[p], table, precision=HIGHEST, preferred_element_type=jnp.float32)
-        if p:
-            part_values = jnp.concatenate(
-                [pltpu.roll(part_values[:, g * LANES : (g + 1) * LANES], p * points, 1) for g in range(3)], axis=1
-            )
-        values = values + part_values
+    transit(planes - 2)
+    finish(planes - 3)
+    lax.fori_loop(planes - 1, planes, drain, 0)
+    finish(planes - 1)
+
     halo[hops] = values[:, :LANES]
     grad_x = values[:, LANES : 2 * LANES]
     grad_y = values[:, 2 * LANES :]
@@ -204,17 +250,15 @@
     copies = [halo_copy(number, h) for number, h in enumerate(offsets)]
     for copy in copies:
         copy.start()
-    grad_z = jnp.dot(halo[hops], depth_ref[hops], precision=HIGHEST, preferred_element_type=jnp.float32)
-    for copy, h in zip(copies, offsets):
+    for copy in copies:
         copy.wait()
-        grad_z = grad_z + jnp.dot(
-            halo[hops - h], depth_ref[hops - h], precision=HIGHEST, preferred_element_type=jnp.float32
-        )
+    around = jnp.concatenate([halo[n] for n in range(2 * hops + 1)], axis=1)
+    grad_z = split_dot(around, depth_ref[...])
     components = (grad_x, grad_y, grad_z)
     quadratic = jnp.zeros_like(grad_x)
     for i in range(3):
         for j in range(3):
-            quadratic = quadratic + metric_ref[i, j] * components[i] * components[j]
+            quadratic = quadratic + metric_ref[i : i + 1, j : j + 1] * components[i] * components[j]
     term = jnp.dot(occ_ref[...], quadratic, precision=HIGHEST, preferred_element_type=jnp.float32)
     terms[me] = jnp.broadcast_to(term, (8, LANES))
 
@@ -231,11 +275,11 @@
     def sent(p, carry):
         core_copy(p).wait_send()
         for t in range(chips - 1):
-            @pl.when(chip < chips - 1 - t)
+            @pl.when((chip < chips - 1 - t) & ((chip > 0) | (p == planes - 1)))
             def _():
                 line_copy(0, p, t, line.at[0, p, t], ahead).wait_send()
 
-            @pl.when(chip > t)
+            @pl.when((chip > t) & ((chip < chips - 1) | (p == planes - 1)))
             def _():
                 line_copy(1, p, t, line.at[1, p, t], behind).wait_send()
         return carry
@@ -260,7 +304,7 @@
     hops = -(-REACH // planes)
     f32 = jnp.float32
     vmem = pl.BlockSpec(memory_space=pltpu.VMEM)
-    hbm = pl.BlockSpec(memory_space=pl.ANY)
+    hbm = pl.BlockSpec(memory_space=pltpu.HBM)
     dma = pltpu.SemaphoreType.DMA
     neighbours = 2 * hops
     rotated, density = pl.pallas_call(
@@ -269,9 +313,15 @@
             jax.ShapeDtypeStruct((planes, owned, plane_size), f32),
             jax.ShapeDtypeStruct((planes, PY * PX), f32),
         ),
-        in_specs=[hbm, hbm, vmem, pl.BlockSpec(memory_space=pltpu.SMEM), vmem, vmem],
+        in_specs=[hbm] * 6,
         out_specs=(vmem, vmem),
         scratch_shapes=[
+            pltpu.VMEM((1, owned), f32),
+            pltpu.VMEM((3, 3), f32),
+            pltpu.VMEM((2 * plane_size, 3 * LANES), jnp.bfloat16),
+            pltpu.VMEM((2 * (neighbours + 1) * LANES, LANES), jnp.bfloat16),
+            pltpu.VMEM((owned, 3 * LANES), f32),
+            dma((4,)),
             pltpu.VMEM((planes, orbital_count, plane_size), f32),
             pltpu.VMEM((orbital_count, window), f32),
             pltpu.VMEM((2 * window, orbital_count), jnp.bfloat16),
@@ -293,15 +343,15 @@
             dma((bands - 1,)),
         ],
         compiler_params=pltpu.CompilerParams(
-            collective_id=0, has_side_effects=True, vmem_limit_bytes=48 * 1024 * 1024
+            collective_id=0, has_side_effects=True, vmem_limit_bytes=62 * 1024 * 1024
         ),
     )(
         jnp.transpose(orbitals, (1, 0, 2)),
         rotation,
         occupation.reshape(1, owned),
         metric,
-        jnp.asarray(plane_tables()),
-        jnp.asarray(depth_tables(planes, hops)),
+        halves(plane_tables()),
+        halves(depth_tables(planes, hops).reshape(-1, LANES)),
     )
     return jnp.transpose(rotated, (1, 0, 2)), density
 

time: 61 us -> 56.9 us (0.933)
  local copies, waits for them, and re-layouts: 6.26 us -> 3.04 us
  Pallas kernels: 53.9 us -> 53 us
    unnamed x12 -> x2, local copies, waits for them, and re-layouts: 6.26 us -> 3.04 us
    pallas_call x1, Pallas kernels: 53.9 us -> 53 us  [local(): pl.pallas_call(functools.partial(kernel, (bands, slabs, planes, owned, ho...]
where the time goes in v2:
time: 56.9 us; the launch traced here: 56.7 us
  Pallas kernels  53 us (93%)
  local copies, waits for them, and re-layouts  3.04 us (5%)
  between operations  0.64 us (1%)
    pallas_call x1, Pallas kernels, local(): pl.pallas_call(functools.partial(kernel, (bands, slabs, planes, owned, ho...  53 us
    unnamed x2, local copies, waits for them, and re-layouts  3.04 us

profile of v2, /device:TPU:0, one launch (start us, length us, event | category | flops | bytes accessed | tf_op | source)
XLA Modules:
  0.0 56.7 jit_solution(5486384825987164071)
XLA Ops:
  0.6 53.0 %shard_map.77 = (f32[6,64,256]{2,1,0:T(8,128)}, f32[6,16]{1,0:T(8,128)}) custom-call(f32[6,1152,256]{2,1,0:T(8,128)} %bitcast.3, f32[1152,512]{1,0:T(8,128)} %rot_hbm.1, f32[1,64]{1,0:T(1,128)} %bitcast.5, f32[3,3]{1,0:T(4,128)} %metric_hbm.1, bf16[512,384]{1,0:T(8,128)(2,1)} %constant.4.clone.plane_hbm, bf16[768,128]{1,0:T(8,128)(2,1)} %constant.5.clone.depth_hbm), custom_call_target="tpu_custom_call" | custom-call | tf_op jit(solution)/shard_map/pallas_call | solution.py:310
  53.7 1.8 %copy.10 = f32[64,6,256]{2,0,1:T(8,128)} copy(f32[64,6,256]{2,0,1:T(8,128)} %bitcast.4) | data formatting | bytes 786432
  55.4 1.3 %copy.11 = f32[6,16]{1,0:T(8,128)} copy(f32[6,16]{1,0:T(8,128)} %get-tuple-element.9) | data formatting | bytes 768

commit v3 on v2

--- a/solution.py
+++ b/solution.py
@@ -13,6 +13,7 @@
 PX = 4
 LANES = 128
 REACH = 6
+WINDOW = 2
 MESH = pl.DeviceIdType.MESH
 STENCIL_WEIGHTS = (6.0 / 7.0, -15.0 / 56.0, 5.0 / 63.0, -1.0 / 56.0, 6.0 / 1925.0, -1.0 / 5544.0)
 HIGHEST = lax.Precision.HIGHEST
@@ -140,22 +141,22 @@
         for t in range(chips - 1):
             @pl.when(chip == 0)
             def _():
-                @pl.when(p > 0)
+                @pl.when(p >= WINDOW)
                 def _():
-                    line_copy(0, p - 1, t, sbuf.at[p - 1, block(chips - 1 - t)], ahead).wait_send()
+                    line_copy(0, p - WINDOW, t, sbuf.at[p - WINDOW, block(chips - 1 - t)], ahead).wait_send()
 
                 line_copy(0, p, t, sbuf.at[p, block(chips - 1 - t)], ahead).start()
 
             @pl.when(chip == chips - 1)
             def _():
-                @pl.when(p > 0)
+                @pl.when(p >= WINDOW)
                 def _():
-                    line_copy(1, p - 1, t, sbuf.at[p - 1, block(t)], behind).wait_send()
+                    line_copy(1, p - WINDOW, t, sbuf.at[p - WINDOW, block(t)], behind).wait_send()
 
                 line_copy(1, p, t, sbuf.at[p, block(t)], behind).start()
         out_ref[p] = sbuf[p, block(chip), :]
 
-    def transit(p):
+    def transit(p, near):
         def rightward(t):
             @pl.when((chip > 0) & (chip < chips - 1 - t))
             def _():
@@ -170,19 +171,15 @@
                 line[1, p, t] += sbuf[p, block(t), :]
                 line_copy(1, p, t, line.at[1, p, t], behind).start()
 
-        @pl.when(chip < chips // 2)
+        @pl.when((chip < chips // 2) if near else (chip >= chips // 2))
         def _():
             for t in range(chips - 1):
                 rightward(t)
+
+        @pl.when((chip >= chips // 2) if near else (chip < chips // 2))
+        def _():
             for t in range(chips - 1):
                 leftward(t)
-
-        @pl.when(chip >= chips // 2)
-        def _():
-            for t in range(chips - 1):
-                leftward(t)
-            for t in range(chips - 1):
-                rightward(t)
 
     def finish(p):
         @pl.when(chip > 0)
@@ -215,25 +212,37 @@
 
         @pl.when(p >= 2)
         def _():
-            transit(p - 2)
+            transit(p - 2, True)
 
         @pl.when(p >= 3)
         def _():
-            finish(p - 3)
+            transit(p - 3, False)
 
         return carry
 
     lax.fori_loop(1, planes, step, 0)
     originate(planes - 1)
 
-    def drain(p, carry):
-        transit(p)
-        finish(p - 1)
+    def early(p, carry):
+        finish(p)
         return carry
 
-    transit(planes - 2)
-    finish(planes - 3)
-    lax.fori_loop(planes - 1, planes, drain, 0)
+    def late(p, carry):
+        transit(p, True)
+        @pl.when(p >= 1)
+        def _():
+            transit(p - 1, False)
+
+        @pl.when(p >= 2)
+        def _():
+            finish(p - 2)
+
+        return carry
+
+    lax.fori_loop(0, max(planes - 4, 0), early, 0)
+    lax.fori_loop(planes - 2, planes, late, 0)
+    transit(planes - 1, False)
+    finish(planes - 2)
     finish(planes - 1)
 
     halo[hops] = values[:, :LANES]
@@ -275,11 +284,11 @@
     def sent(p, carry):
         core_copy(p).wait_send()
         for t in range(chips - 1):
-            @pl.when((chip < chips - 1 - t) & ((chip > 0) | (p == planes - 1)))
+            @pl.when((chip < chips - 1 - t) & ((chip > 0) | (p >= planes - WINDOW)))
             def _():
                 line_copy(0, p, t, line.at[0, p, t], ahead).wait_send()
 
-            @pl.when((chip > t) & ((chip < chips - 1) | (p == planes - 1)))
+            @pl.when((chip > t) & ((chip < chips - 1) | (p >= planes - WINDOW)))
             def _():
                 line_copy(1, p, t, line.at[1, p, t], behind).wait_send()
         return carry

time: 56.9 us -> 55 us (0.967)
  Pallas kernels: 53 us -> 51.1 us
    pallas_call x1, Pallas kernels: 53 us -> 51.1 us  [local(): pl.pallas_call(functools.partial(kernel, (bands, slabs, planes, owned, ho...]
where the time goes in v3:
time: 55 us; the launch traced here: 54.8 us
  Pallas kernels  51.1 us (93%)
  local copies, waits for them, and re-layouts  3.04 us (6%)
  between operations  0.64 us (1%)
    pallas_call x1, Pallas kernels, local(): pl.pallas_call(functools.partial(kernel, (bands, slabs, planes, owned, ho...  51.1 us
    unnamed x2, local copies, waits for them, and re-layouts  3.04 us

profile of v3, /device:TPU:0, one launch (start us, length us, event | category | flops | bytes accessed | tf_op | source)
XLA Modules:
  0.0 54.8 jit_solution(13514134389157885226)
XLA Ops:
  0.6 51.1 %shard_map.77 = (f32[6,64,256]{2,1,0:T(8,128)}, f32[6,16]{1,0:T(8,128)}) custom-call(f32[6,1152,256]{2,1,0:T(8,128)} %bitcast.3, f32[1152,512]{1,0:T(8,128)} %rot_hbm.1, f32[1,64]{1,0:T(1,128)} %bitcast.5, f32[3,3]{1,0:T(4,128)} %metric_hbm.1, bf16[512,384]{1,0:T(8,128)(2,1)} %constant.4.clone.plane_hbm, bf16[768,128]{1,0:T(8,128)(2,1)} %constant.5.clone.depth_hbm), custom_call_target="tpu_custom_call" | custom-call | tf_op jit(solution)/shard_map/pallas_call | solution.py:319
  51.8 1.8 %copy.10 = f32[64,6,256]{2,0,1:T(8,128)} copy(f32[64,6,256]{2,0,1:T(8,128)} %bitcast.4) | data formatting | bytes 786432
  53.5 1.3 %copy.11 = f32[6,16]{1,0:T(8,128)} copy(f32[6,16]{1,0:T(8,128)} %get-tuple-element.9) | data formatting | bytes 768

commit v4 on v3

--- a/solution.py
+++ b/solution.py
@@ -210,13 +210,13 @@
         core_copy(p).start()
         originate(p - 1)
 
-        @pl.when(p >= 2)
-        def _():
-            transit(p - 2, True)
-
         @pl.when(p >= 3)
         def _():
-            transit(p - 3, False)
+            transit(p - 3, True)
+
+        @pl.when(p >= 4)
+        def _():
+            transit(p - 4, False)
 
         return carry
 
@@ -239,8 +239,8 @@
 
         return carry
 
-    lax.fori_loop(0, max(planes - 4, 0), early, 0)
-    lax.fori_loop(planes - 2, planes, late, 0)
+    lax.fori_loop(0, max(planes - 5, 0), early, 0)
+    lax.fori_loop(planes - 3, planes, late, 0)
     transit(planes - 1, False)
     finish(planes - 2)
     finish(planes - 1)

time: 55 us -> 55 us (level)
  no operation moved by 1% of the time
where the time goes in v4:
time: 55 us; the launch traced here: 54.8 us
  Pallas kernels  51.1 us (93%)
  local copies, waits for them, and re-layouts  3.04 us (6%)
  between operations  0.64 us (1%)
    pallas_call x1, Pallas kernels, local(): pl.pallas_call(functools.partial(kernel, (bands, slabs, planes, owned, ho...  51.1 us
    unnamed x2, local copies, waits for them, and re-layouts  3.04 us

profile of v4, /device:TPU:0, one launch (start us, length us, event | category | flops | bytes accessed | tf_op | source)
XLA Modules:
  0.0 54.8 jit_solution(1269540484319636605)
XLA Ops:
  0.6 51.1 %shard_map.77 = (f32[6,64,256]{2,1,0:T(8,128)}, f32[6,16]{1,0:T(8,128)}) custom-call(f32[6,1152,256]{2,1,0:T(8,128)} %bitcast.3, f32[1152,512]{1,0:T(8,128)} %rot_hbm.1, f32[1,64]{1,0:T(1,128)} %bitcast.5, f32[3,3]{1,0:T(4,128)} %metric_hbm.1, bf16[512,384]{1,0:T(8,128)(2,1)} %constant.4.clone.plane_hbm, bf16[768,128]{1,0:T(8,128)(2,1)} %constant.5.clone.depth_hbm), custom_call_target="tpu_custom_call" | custom-call | tf_op jit(solution)/shard_map/pallas_call | solution.py:319
  51.8 1.8 %copy.10 = f32[64,6,256]{2,0,1:T(8,128)} copy(f32[64,6,256]{2,0,1:T(8,128)} %bitcast.4) | data formatting | bytes 786432
  53.6 1.3 %copy.11 = f32[6,16]{1,0:T(8,128)} copy(f32[6,16]{1,0:T(8,128)} %get-tuple-element.9) | data formatting | bytes 768
